TPU v7x, 32 devices: a whole 2x2x4 slice. The times are simulated.
32 devices in a mesh: gx: 8 (over y, x, core), gy: 4 (over z).
Axes of the slice: x: 2, y: 2, z: 4, core: 2. Of those that a mesh axis runs over, the one named last changes fastest.
Arguments:
- activations: bfloat16 [1024, 7168], P('gx', 'gy'), may hold values from -6 to 6
- out_grad: bfloat16 [1024, 7168], P('gx', 'gy'), may hold values from -0.59765625 to 0.59765625
- saved_gate: bfloat16 [1024, 2, 1024], P('gx', None, 'gy'), may hold values from -9 to 9
- saved_up: bfloat16 [1024, 2, 1024], P('gx', None, 'gy'), may hold values from -6 to 6
- route_ids: int32 [1024, 2], P('gx'), may hold values from 0 to 7, all different within a row; in each aligned block of 128 rows (0 to 127, 128 to 255, ...) at most 48 rows name the same one
- route_weight: float32 [1024, 2], P('gx'), may hold values from 0.1 to 1
- down_weight: bfloat16 [8, 1024, 7168], P('gx', None, 'gy'), may hold values from -0.1875 to 0.1875
Outputs:
- grad_gate: bfloat16 [8, 7168, 1024], P('gx', 'gy')
- grad_up: bfloat16 [8, 7168, 1024], P('gx', 'gy')
- grad_down: bfloat16 [8, 1024, 7168], P('gx', None, 'gy')
Inputs may be any that keep to these rules, and one draw needn't show every extreme that they name: `route_ids`: each token names 2 different experts. Within each aligned block of 128 tokens (one index of gx) no expert is named by more than 48 tokens, a bound that some block reaches.
All inputs are finite; a program needn't handle non-finite values.
Results may differ from a plain program's by a relative error of at most 0.02.
Values may be sent and summed in bfloat16 or wider, within the bound.
A program may use at most 64 MiB of HBM per device.

v0:
```python
import jax
import jax.numpy as jnp
from jax import lax
from jax.sharding import PartitionSpec as P

MOST = 48


def local_grads(hidden_grad, gate_rows, up_rows):
    gate_val = gate_rows.astype(jnp.float32)
    up_val = up_rows.astype(jnp.float32)
    gate_sig = jax.nn.sigmoid(gate_val)
    silu_val = gate_val * gate_sig
    hidden_act = (silu_val * up_val).astype(jnp.bfloat16)
    grad_upper = (hidden_grad * silu_val).astype(jnp.bfloat16)
    grad_gated = (hidden_grad * up_val * gate_sig * (1.0 + gate_val * (1.0 - gate_sig))).astype(
        jnp.bfloat16
    )
    return (hidden_act, grad_gated, grad_upper)


def contract_rows(left, right):
    return lax.dot_general(
        left, right, (((0,), (0,)), ((), ())), preferred_element_type=jnp.float32
    ).astype(jnp.bfloat16)


def slot_rows(route_ids, experts):
    flat_ids = route_ids.reshape(-1)
    onehot = (flat_ids[:, None] == jnp.arange(experts, dtype=jnp.int32)[None, :]).astype(jnp.int32)
    rank_in = jnp.sum((jnp.cumsum(onehot, axis=0) - onehot) * onehot, axis=1)
    return flat_ids * MOST + rank_in


def pack_rows(values, target, experts):
    buffer = jnp.zeros((experts * MOST, values.shape[-1]), values.dtype).at[target].set(values)
    return buffer.reshape(experts, MOST, values.shape[-1])


def merge_rows(values):
    return values.reshape(-1, values.shape[-1])


def on_device(activations, out_grad, saved_gate, saved_up, route_ids, route_weight, down_weight):
    experts = lax.axis_size("gx")
    top_count = route_ids.shape[1]
    target = slot_rows(route_ids, experts)
    act_routes = pack_rows(jnp.repeat(activations, top_count, axis=0), target, experts)
    scaled = (
        route_weight.reshape(-1, 1) * jnp.repeat(out_grad, top_count, axis=0).astype(jnp.float32)
    ).astype(jnp.bfloat16)
    grad_routes = pack_rows(scaled, target, experts)
    gate_routes = pack_rows(saved_gate.reshape(-1, saved_gate.shape[-1]), target, experts)
    up_routes = pack_rows(saved_up.reshape(-1, saved_up.shape[-1]), target, experts)
    rows_act, rows_grad, gate_rows, up_rows = (
        lax.all_to_all(act_routes, "gx", split_axis=0, concat_axis=0, tiled=True),
        lax.all_to_all(grad_routes, "gx", split_axis=0, concat_axis=0, tiled=True),
        lax.all_to_all(gate_routes, "gx", split_axis=0, concat_axis=0, tiled=True),
        lax.all_to_all(up_routes, "gx", split_axis=0, concat_axis=0, tiled=True),
    )
    rows_grad = merge_rows(rows_grad)
    gate_rows = merge_rows(gate_rows)
    up_rows = merge_rows(up_rows)
    weight = down_weight[0]
    partial_value = lax.dot_general(
        rows_grad, weight, (((1,), (1,)), ((), ())), preferred_element_type=jnp.float32
    )
    rows_act = merge_rows(rows_act)
    hidden_grad = lax.psum(partial_value.astype(jnp.bfloat16), "gy").astype(jnp.float32)
    gate_full, up_full = (
        lax.all_gather(gate_rows, "gy", axis=1, tiled=True),
        lax.all_gather(up_rows, "gy", axis=1, tiled=True),
    )
    hidden_act, grad_gated, grad_upper = local_grads(hidden_grad, gate_full, up_full)
    grad_gate = contract_rows(rows_act, grad_gated)[None]
    grad_up = contract_rows(rows_act, grad_upper)[None]
    grad_down = contract_rows(hidden_act, rows_grad)[None]
    return (grad_gate, grad_up, grad_down)


def solution(mesh):
    placed = (
        P("gx", "gy"),
        P("gx", "gy"),
        P("gx", None, "gy"),
        P("gx", None, "gy"),
        P("gx", None),
        P("gx", None),
        P("gx", None, "gy"),
    )
    return jax.shard_map(
        on_device,
        mesh=mesh,
        in_specs=placed,
        out_specs=(P("gx", "gy", None), P("gx", "gy", None), P("gx", None, "gy")),
        check_vma=False,
    )
```

profile of v0, /device:TPU:6, one launch (start us, length us, event | category | flops | bytes accessed | tf_op | source)
XLA Modules:
  0.0 143.3 jit_solution(7677745777979854261)
XLA Ops:
  7.2 0.0 copy-start.3
  7.2 0.0 copy-start.1
  7.2 0.7 broadcast_multiply_fusion
  7.9 0.8 copy.11
  8.7 0.1 eq.29
  8.8 0.1 eq.25
  9.0 0.1 copy.10
  9.1 0.1 mul.52
  9.3 0.6 reduce-window.6
  9.8 0.2 slice_reduce_fusion
  10.1 1.0 reshape.129
  11.1 0.1 fusion.31
  11.2 2.1 %scatter_custom_fusion.3 = bf16[384,256]{1,0:T(8,128)(2,1)} fusion(s32[256]{0:T(256)S(1)} %bitcast.42, bf16[256,256]{1,0:T(8,128)(2,1)S(1)} %reshape.129, bf16[]{:T(256)} %constant.5.clone.1), kind=kCustom, calls=%fused_computation.35 | custom fusion | bytes 196610 | tf_op jit(solution)/shard_map/scatter | solution.py:36
  13.3 4.2 %all-to-all-start.3 = ((bf16[8,48,256]{2,1,0:T(8,128)(2,1)}), bf16[8,48,256]{2,1,0:T(8,128)(2,1)S(1)}, u32[]{:S(2)}, u32[]{:S(2)}) async-start(bf16[8,48,256]{2,1,0:T(8,128)(2,1)} %bitcast.11), calls=%async_computation.3 | async-start | bytes 393216 | tf_op jit(solution)/shard_map/all_to_all | solution.py:58
  17.5 1.0 reshape.121
  18.4 2.1 %scatter_custom_fusion.2 = bf16[384,256]{1,0:T(8,128)(2,1)} fusion(s32[256]{0:T(256)S(1)} %bitcast.43, bf16[256,256]{1,0:T(8,128)(2,1)S(1)} %reshape.121, bf16[]{:T(256)} %constant.5.clone.1), kind=kCustom, calls=%fused_computation.37 | custom fusion | bytes 196610 | tf_op jit(solution)/shard_map/scatter | solution.py:36
  20.5 0.8 all-to-all-done.3
  21.3 0.0 copy-start
  21.3 0.7 copy-done
  22.0 5.7 %all-to-all-start.2 = ((bf16[8,48,256]{2,1,0:T(8,128)(2,1)}), bf16[8,48,256]{2,1,0:T(8,128)(2,1)S(1)}, u32[]{:S(2)}, u32[]{:S(2)}) async-start(bf16[8,48,256]{2,1,0:T(8,128)(2,1)} %bitcast.9), calls=%async_computation.2 | async-start | bytes 393216 | tf_op jit(solution)/shard_map/all_to_all | solution.py:59
  27.7 0.0 copy-done.3
  27.7 0.1 copy.13
  27.8 0.1 mul.54
  27.9 0.0 copy-done.1
  28.0 1.7 %broadcast_in_dim.21 = f32[128,2,1792]{2,1,0:T(2,128)} broadcast(bf16[128,1792]{1,0:T(8,128)(2,1)S(1)} %copy-done.1), dimensions={0,2} | broadcast | bytes 2293760 | tf_op jit(solution)/shard_map/broadcast_in_dim | solution.py:50
  29.7 2.5 %convert_element_type.50 = f32[256,1792]{1,0:T(8,128)S(1)} reshape(f32[128,2,1792]{2,1,0:T(2,128)} %broadcast_in_dim.21) | data formatting | bytes 3670016 | tf_op jit(solution)/shard_map/convert_element_type | solution.py:50
  32.2 3.2 %scatter_custom_fusion.1 = bf16[384,1792]{1,0:T(8,128)(2,1)} fusion(s32[256]{0:T(256)S(1)} %bitcast.44, f32[256,1792]{1,0:T(8,128)S(1)} %convert_element_type.50, f32[256]{0:T(256)S(1)} %mul.54, bf16[]{:T(256)} %constant.5.clone.1), kind=kCustom, calls=%fused_computation.29 | custom fusion | flops 917504 | bytes 3212290 | tf_op jit(solution)/shard_map/scatter | solution.py:36
  35.4 0.0 copy-start.2
  35.4 0.0 all-to-all-done.2
  35.5 4.3 %all-to-all-start.1 = ((bf16[8,48,1792]{2,1,0:T(8,128)(2,1)}), bf16[8,48,1792]{2,1,0:T(8,128)(2,1)S(1)}, u32[]{:S(2)}, u32[]{:S(2)}) async-start(bf16[8,48,1792]{2,1,0:T(8,128)(2,1)} %bitcast.6), calls=%async_computation.1 | async-start | bytes 2752512 | tf_op jit(solution)/shard_map/all_to_all | solution.py:57
  39.8 0.0 copy-done.2
  39.8 0.5 broadcast_in_dim.20
  40.3 0.3 reshape.105
  40.6 3.2 %scatter_custom_fusion = bf16[384,1792]{1,0:T(8,128)(2,1)} fusion(s32[256]{0:T(256)S(1)} %bitcast.45, bf16[256,1792]{1,0:T(8,128)(2,1)S(1)} %reshape.105, bf16[]{:T(256)} %constant.5.clone.1), kind=kCustom, calls=%fused_computation.33 | custom fusion | bytes 1376258 | tf_op jit(solution)/shard_map/scatter | solution.py:36
  43.8 20.0 %all_gather.7 = bf16[384,1024]{1,0:T(8,128)(2,1)S(1)} all-gather(bf16[384,256]{1,0:T(8,128)(2,1)} %bitcast.40), channel_id=1, replica_groups=mesh['gx'=8,'gy'=4] {'gy'}, dimensions={1}, use_global_device_ids=true | all-gather | bytes 983040 | tf_op jit(solution)/shard_map/all_gather | solution.py:71
  63.8 0.0 all-to-all-done.1
  63.8 4.2 %all-to-all-start = ((bf16[8,48,1792]{2,1,0:T(8,128)(2,1)}), bf16[8,48,1792]{2,1,0:T(8,128)(2,1)}, u32[]{:S(2)}, u32[]{:S(2)}) async-start(bf16[8,48,1792]{2,1,0:T(8,128)(2,1)} %bitcast.4), calls=%async_computation | async-start | bytes 2752512 | tf_op jit(solution)/shard_map/all_to_all | solution.py:56
  68.1 0.0 all-reduce.2.cloned.1.call-start
  68.1 4.5 %fusion.14 = bf16[384,1024]{1,0:T(8,128)(2,1)} fusion(bf16[384,1792]{1,0:T(8,128)(2,1)S(1)} %bitcast.37, bf16[1,1024,1792]{2,1,0:T(8,128)(2,1)} %param.13), kind=kOutput, calls=%fused_computation.28 | convolution fusion | flops 1409679360 | bytes 5832704 | tf_op jit(solution)/shard_map/dot_general | solution.py:65
  72.6 0.0 all-reduce.2.cloned.1.call-update
  72.7 27.1 %all_gather.6 = bf16[384,1024]{1,0:T(8,128)(2,1)S(1)} all-gather(bf16[384,256]{1,0:T(8,128)(2,1)S(1)} %bitcast.39), channel_id=1, replica_groups=mesh['gx'=8,'gy'=4] {'gy'}, dimensions={1}, use_global_device_ids=true | all-gather | bytes 983040 | tf_op jit(solution)/shard_map/all_gather | solution.py:72
  99.8 4.0 %fusion.4 = bf16[1,1024,1792]{2,1,0:T(8,128)(2,1)} fusion(bf16[384,1792]{1,0:T(8,128)(2,1)S(1)} %bitcast.38, bf16[384,1024]{1,0:T(8,128)(2,1)S(1)} %all_gather.6, bf16[384,1024]{1,0:T(8,128)(2,1)S(1)} %all_gather.7), kind=kOutput, calls=%fused_computation.11 | convolution fusion | flops 1414266880 | bytes 6619136 | tf_op jit(solution)/shard_map/dot_general | solution.py:23
  103.8 0.0 all-to-all-done
  103.8 21.5 %all-reduce.2.cloned.1.call-done = bf16[384,1024]{1,0:T(8,128)(2,1)} async-done(((bf16[384,1024]{1,0:T(8,128)(2,1)}), bf16[384,1024]{1,0:T(8,128)(2,1)}) %all-reduce.2.cloned.1.call-update) | async-done | bytes 786448 | tf_op jit(solution)/shard_map/psum | solution.py:69
  125.3 0.0 copy-start.4
  125.3 5.8 %fusion.2 = bf16[1,1792,1024]{2,1,0:T(8,128)(2,1)} fusion(bf16[384,1792]{1,0:T(8,128)(2,1)} %bitcast.5, bf16[384,1024]{1,0:T(8,128)(2,1)S(1)} %all_gather.6, bf16[384,1024]{1,0:T(8,128)(2,1)} %all-reduce.2.cloned.1.call-done, bf16[384,1024]{1,0:T(8,128)(2,1)S(1)} %all_gather.7), kind=kOutput, calls=%fused_computation.9 | convolution fusion | flops 1416232960 | bytes 7405568 | tf_op jit(solution)/shard_map/dot_general | solution.py:23
  131.1 0.0 copy-done.4
  131.1 5.4 %fusion.3 = bf16[1,1792,1024]{2,1,0:T(8,128)(2,1)} fusion(bf16[384,1792]{1,0:T(8,128)(2,1)} %bitcast.5, bf16[384,1024]{1,0:T(8,128)(2,1)S(1)} %copy-done.4, bf16[384,1024]{1,0:T(8,128)(2,1)S(1)} %all_gather.7), kind=kOutput, calls=%fused_computation.10 | convolution fusion | flops 1414266880 | bytes 6619136 | tf_op jit(solution)/shard_map/dot_general | solution.py:23
  (4 shorter events, 0.1 us)
Async XLA Ops:
  7.2 20.5 %copy-start.3 = (f32[128,2]{0,1:T(2,128)S(1)}, f32[128,2]{0,1:T(2,128)}, u32[]{:S(2)}) copy-start(f32[128,2]{0,1:T(2,128)} %param.12) | copy-start | bytes 3076
  7.2 20.8 %copy-start.1 = (bf16[128,1792]{1,0:T(8,128)(2,1)S(1)}, bf16[128,1792]{1,0:T(8,128)(2,1)}, u32[]{:S(2)}) copy-start(bf16[128,1792]{1,0:T(8,128)(2,1)} %param.8) | copy-start | bytes 1376260
  13.3 8.0 %all-to-all-start.3 = ((bf16[8,48,256]{2,1,0:T(8,128)(2,1)}), bf16[8,48,256]{2,1,0:T(8,128)(2,1)S(1)}, u32[]{:S(2)}, u32[]{:S(2)}) async-start(bf16[8,48,256]{2,1,0:T(8,128)(2,1)} %bitcast.11), calls=%async_computation.3 | async-start | bytes 393216 | tf_op jit(solution)/shard_map/all_to_all | solution.py:58
  21.3 0.7 copy-start
  22.0 13.5 %all-to-all-start.2 = ((bf16[8,48,256]{2,1,0:T(8,128)(2,1)}), bf16[8,48,256]{2,1,0:T(8,128)(2,1)S(1)}, u32[]{:S(2)}, u32[]{:S(2)}) async-start(bf16[8,48,256]{2,1,0:T(8,128)(2,1)} %bitcast.9), calls=%async_computation.2 | async-start | bytes 393216 | tf_op jit(solution)/shard_map/all_to_all | solution.py:59
  35.4 4.3 %copy-start.2 = (bf16[128,1792]{1,0:T(8,128)(2,1)S(1)}, bf16[128,1792]{1,0:T(8,128)(2,1)}, u32[]{:S(2)}) copy-start(bf16[128,1792]{1,0:T(8,128)(2,1)} %param.7) | copy-start | bytes 1376260
  35.5 28.4 %all-to-all-start.1 = ((bf16[8,48,1792]{2,1,0:T(8,128)(2,1)}), bf16[8,48,1792]{2,1,0:T(8,128)(2,1)S(1)}, u32[]{:S(2)}, u32[]{:S(2)}) async-start(bf16[8,48,1792]{2,1,0:T(8,128)(2,1)} %bitcast.6), calls=%async_computation.1 | async-start | bytes 2752512 | tf_op jit(solution)/shard_map/all_to_all | solution.py:57
  63.8 40.0 %all-to-all-start = ((bf16[8,48,1792]{2,1,0:T(8,128)(2,1)}), bf16[8,48,1792]{2,1,0:T(8,128)(2,1)}, u32[]{:S(2)}, u32[]{:S(2)}) async-start(bf16[8,48,1792]{2,1,0:T(8,128)(2,1)} %bitcast.4), calls=%async_computation | async-start | bytes 2752512 | tf_op jit(solution)/shard_map/all_to_all | solution.py:56
  68.1 57.3 %all-reduce.2.cloned.1.call-start = ((), (), s32[]{:S(2)}) async-start(), calls=%async_computation.4 | async-start | bytes 1572864 | tf_op jit(solution)/shard_map/psum | solution.py:69
  125.3 5.8 %copy-start.4 = (bf16[384,1024]{1,0:T(8,128)(2,1)S(1)}, bf16[384,1024]{1,0:T(8,128)(2,1)}, u32[]{:S(2)}) copy-start(bf16[384,1024]{1,0:T(8,128)(2,1)} %all-reduce.2.cloned.1.call-done) | copy-start | bytes 2359300
Sparse Core Ops, SparseCore 0:
  72.8 52.4 all-reduce.1
where the time goes:
time: 146 us; the launch traced here: 143 us
  blocking collectives  47.1 us (32%)
  waiting for transfers between devices  22.3 us (15%)
  matrix products  19.7 us (13%)
  starting transfers between devices  18.5 us (13%)
  local copies, waits for them, and re-layouts  16.9 us (12%)
  between operations  14.1 us (10%)
  other arithmetic  4.7 us (3%)
    all_gather x1, blocking collectives, on_device(): lax.all_gather(up_rows, 'gy', axis=1, tiled=True)  27.1 us
    psum x1, waiting for transfers between devices, on_device(): lax.psum(partial_value.astype(jnp.bfloat16), 'gy').astype(jnp.float32)  21.5 us
    all_gather x1, blocking collectives, on_device(): lax.all_gather(gate_rows, 'gy', axis=1, tiled=True)  20 us
    dot_general x3, matrix products, contract_rows(): lax.dot_general(left, right, (((0,), (0,)), ((), ())), preferred_element_...  15.2 us
    scatter x3, local copies, waits for them, and re-layouts, pack_rows(): jnp.zeros((experts * MOST, values.shape[-1]), values.dtype).at[target]  7.38 us
    all_to_all x1, starting transfers between devices, on_device(): lax.all_to_all(up_routes, 'gx', split_axis=0, concat_axis=0, tiled=True)  5.69 us
    dot_general x1, matrix products, on_device(): lax.dot_general(rows_grad, weight, (((1,), (1,)), ((), ())), preferred_el...  4.54 us
    all_to_all x1, starting transfers between devices, on_device(): lax.all_to_all(grad_routes, 'gx', split_axis=0, concat_axis=0, tiled=True)  4.33 us
  transfers between devices with their start and end apart: 5, of which 2 were waited for; matrix products, arithmetic and copies ran while one was open for 16% of the time, Pallas kernels for 0%

commit v1 on v0

v1 whole, which is shorter than its diff:
```python
import functools

import jax
import jax.numpy as jnp
from jax import lax
from jax.experimental import pallas as pl
from jax.experimental.pallas import tpu as pltpu
from jax.sharding import PartitionSpec as P

MOST = 48
F32 = jnp.float32
BF16 = jnp.bfloat16
MESH = pl.DeviceIdType.MESH


def contract_rows(left, right):
    return lax.dot_general(
        left, right, (((0,), (0,)), ((), ())), preferred_element_type=jnp.float32
    ).astype(jnp.bfloat16)


def dot(left, right):
    return jnp.dot(left, right, preferred_element_type=F32)


def exchange_kernel(
    n_gx,
    n_gy,
    top,
    act_ref,
    grad_ref,
    pre_ref,
    ids_ref,
    wt_ref,
    down_hbm,
    rows_act,
    rows_grad,
    ha_ref,
    gg_ref,
    gu_ref,
    down,
    act_send,
    grad_send,
    pre_all,
    pre_send,
    pre_rows,
    part,
    part_in,
    hid,
    fac_gate,
    fac_up,
    down_sem,
    act_ss,
    act_rs,
    grad_ss,
    grad_rs,
    all_ss,
    all_rs,
    pre_ss,
    pre_rs,
    part_ss,
    part_rs,
    hid_ss,
    hid_rs,
):
    me = lax.axis_index("gx")
    my = lax.axis_index("gy")
    tokens = act_ref.shape[0]
    routes = tokens * top
    slots = n_gx * MOST
    per = n_gx // n_gy
    block = per * MOST
    share = pre_ref.shape[1] // 2

    def to_gx(src, dst, ss, rs, other):
        return pltpu.make_async_remote_copy(
            src_ref=src, dst_ref=dst, send_sem=ss, recv_sem=rs,
            device_id={"gx": other}, device_id_type=MESH,
        )

    def to_gy(src, dst, ss, rs, other):
        return pltpu.make_async_remote_copy(
            src_ref=src, dst_ref=dst, send_sem=ss, recv_sem=rs,
            device_id={"gy": other}, device_id_type=MESH,
        )

    barrier = pltpu.get_barrier_semaphore()
    for d in range(1, n_gx):
        pl.semaphore_signal(
            barrier, inc=1, device_id={"gx": lax.rem(me + d, n_gx)}, device_id_type=MESH
        )
    for d in range(1, n_gy):
        pl.semaphore_signal(
            barrier, inc=1, device_id={"gy": lax.rem(my + d, n_gy)}, device_id_type=MESH
        )
    down_copy = pltpu.make_async_copy(down_hbm, down, down_sem)
    down_copy.start()
    pl.semaphore_wait(barrier, n_gx - 1 + n_gy - 1)

    for d in range(1, n_gy):
        other = lax.rem(my + d, n_gy)
        to_gy(pre_ref, pre_all.at[my], all_ss.at[d], all_rs.at[my], other).start()
    pre_all[my] = pre_ref[...]

    ids = ids_ref[...]
    height = max(n_gx, 16)
    expert = lax.broadcasted_iota(jnp.int32, (height, routes), 0)
    named = (expert == ids).astype(F32)
    before = lax.broadcasted_iota(jnp.int32, (tokens, tokens), 0)
    after = lax.broadcasted_iota(jnp.int32, (tokens, tokens), 1)
    less = (before < after).astype(F32).astype(BF16)
    upto = (before <= after).astype(F32).astype(BF16)
    named_low = named.astype(BF16)
    counts = []
    for kb in range(top):
        total = jnp.zeros((height, tokens), F32)
        for ka in range(top):
            total += dot(
                named_low[:, ka * tokens : (ka + 1) * tokens], upto if ka < kb else less
            )
        counts.append(total)
    count = jnp.concatenate(counts, axis=1)
    rank = jnp.sum(count * named, axis=0, keepdims=True)
    slot = ids * MOST + rank.astype(jnp.int32)
    places = lax.broadcasted_iota(jnp.int32, (slots, routes), 0)
    chosen = places == slot
    pick = chosen.astype(F32)
    weight = jnp.sum(pick * wt_ref[...], axis=1, keepdims=True)
    pick_tok = pick[:, :tokens]
    for k in range(1, top):
        pick_tok = pick_tok + pick[:, k * tokens : (k + 1) * tokens]
    pick_tok = pick_tok.astype(BF16)
    pick = pick.astype(BF16)

    width = grad_ref.shape[1]
    grad_send[...] = (
        (dot(pick_tok, grad_ref[...]) * weight).astype(BF16).reshape(n_gx, MOST, width)
    )
    for d in range(1, n_gx):
        other = lax.rem(me + d, n_gx)
        to_gx(
            grad_send.at[other], rows_grad.at[me], grad_ss.at[d], grad_rs.at[me], other
        ).start()
    rows_grad[me] = grad_send[me]

    act_send[...] = dot(pick_tok, act_ref[...]).astype(BF16).reshape(n_gx, MOST, width)
    for d in range(1, n_gx):
        other = lax.rem(me + d, n_gx)
        to_gx(
            act_send.at[other], rows_act.at[me], act_ss.at[d], act_rs.at[me], other
        ).start()
    rows_act[me] = act_send[me]

    down_copy.wait()
    home = me // per
    for i in range(n_gy):
        q = lax.rem(home + n_gy - i, n_gy)
        for j in range(per):
            s = q * per + j

            @pl.when(s != me)
            def _():
                to_gx(
                    grad_send.at[0], rows_grad.at[s], grad_ss.at[0], grad_rs.at[s], me
                ).wait_recv()

        rows = rows_grad[pl.ds(q * per, per)].reshape(block, width)
        value = lax.dot_general(
            rows, down[...], (((1,), (1,)), ((), ())), preferred_element_type=F32
        ).astype(BF16)
        part[q] = value

        @pl.when(q != my)
        def _():
            to_gy(part.at[q], part_in.at[my], part_ss.at[q], part_rs.at[my], q).start()

        @pl.when(q == my)
        def _():
            part_in[my] = part[q]

    for d in range(1, n_gy):
        other = lax.rem(my + d, n_gy)
        to_gy(pre_ref, pre_all.at[other], all_ss.at[0], all_rs.at[other], my).wait_recv()
    for y in range(n_gy):
        pre_send[:, y] = (
            dot(pick, pre_all[y]).astype(BF16).reshape(n_gx, MOST, 2 * share)
        )
    for d in range(1, n_gx):
        other = lax.rem(me + d, n_gx)
        to_gx(
            pre_send.at[other], pre_rows.at[me], pre_ss.at[d], pre_rs.at[me], other
        ).start()
    pre_rows[me] = pre_send[me]

    for d in range(1, n_gy):
        other = lax.rem(my + d, n_gy)
        to_gy(part.at[0], part_in.at[other], part_ss.at[0], part_rs.at[other], my).wait_recv()
    total = part_in[0].astype(F32)
    for y in range(1, n_gy):
        total = total + part_in[y].astype(F32)
    hid[my] = total.astype(BF16)
    for d in range(1, n_gy):
        other = lax.rem(my + d, n_gy)
        to_gy(hid.at[my], hid.at[my], hid_ss.at[d], hid_rs.at[my], other).start()

    for d in range(1, n_gx):
        other = lax.rem(me + d, n_gx)
        to_gx(pre_send.at[0], pre_rows.at[other], pre_ss.at[0], pre_rs.at[other], me).wait_recv()
    for q in range(n_gy):
        for y in range(n_gy):
            both = pre_rows[q * per : (q + 1) * per, y].reshape(block, 2 * share).astype(F32)
            gate, up = both[:, :share], both[:, share:]
            sig = jax.nn.sigmoid(gate)
            silu = gate * sig
            cols = slice(y * share, (y + 1) * share)
            ha_ref[q, :, cols] = (silu * up).astype(BF16)
            fac_up[q, :, cols] = silu
            fac_gate[q, :, cols] = up * sig * (1.0 + gate * (1.0 - sig))

    for d in range(1, n_gy):
        other = lax.rem(my + d, n_gy)
        to_gy(hid.at[0], hid.at[other], hid_ss.at[0], hid_rs.at[other], my).wait_recv()
    for q in range(n_gy):
        value = hid[q].astype(F32)
        gg_ref[q] = (value * fac_gate[q]).astype(BF16)
        gu_ref[q] = (value * fac_up[q]).astype(BF16)

    for d in range(1, n_gx):
        other = lax.rem(me + d, n_gx)
        to_gx(act_send.at[0], rows_act.at[other], act_ss.at[0], act_rs.at[other], me).wait_recv()
    for d in range(1, n_gx):
        other = lax.rem(me + d, n_gx)
        for src, dst, ss, rs in (
            (grad_send, rows_grad, grad_ss, grad_rs),
            (act_send, rows_act, act_ss, act_rs),
            (pre_send, pre_rows, pre_ss, pre_rs),
        ):
            to_gx(src.at[other], dst.at[me], ss.at[d], rs.at[me], other).wait_send()
    for d in range(1, n_gy):
        other = lax.rem(my + d, n_gy)
        to_gy(pre_ref, pre_all.at[my], all_ss.at[d], all_rs.at[my], other).wait_send()
        to_gy(part.at[other], part_in.at[my], part_ss.at[other], part_rs.at[my], other).wait_send()
        to_gy(hid.at[my], hid.at[my], hid_ss.at[d], hid_rs.at[my], other).wait_send()


def on_device(activations, out_grad, saved_gate, saved_up, route_ids, route_weight, down_weight):
    n_gx, n_gy = lax.axis_size("gx"), lax.axis_size("gy")
    tokens, top = route_ids.shape
    routes, slots = tokens * top, n_gx * MOST
    width, share = activations.shape[1], saved_gate.shape[2]
    hidden = down_weight.shape[1]
    rows = slots // n_gy
    ids = route_ids.T.reshape(1, routes)
    wt = route_weight.T.reshape(1, routes)
    pre = jnp.concatenate([saved_gate, saved_up], axis=2)
    pre = pre.transpose(1, 0, 2).reshape(routes, 2 * share)
    vmem = pl.BlockSpec(memory_space=pltpu.VMEM)
    dma = pltpu.SemaphoreType.DMA
    shape = jax.ShapeDtypeStruct
    rows_act, rows_grad, ha, gg, gu = pl.pallas_call(
        functools.partial(exchange_kernel, n_gx, n_gy, top),
        out_shape=(
            shape((n_gx, MOST, width), BF16),
            shape((n_gx, MOST, width), BF16),
            shape((n_gy, rows, hidden), BF16),
            shape((n_gy, rows, hidden), BF16),
            shape((n_gy, rows, hidden), BF16),
        ),
        in_specs=[vmem] * 5 + [pl.BlockSpec(memory_space=pl.ANY)],
        out_specs=[vmem] * 5,
        scratch_shapes=[
            pltpu.VMEM((hidden, width), BF16),
            pltpu.VMEM((n_gx, MOST, width), BF16),
            pltpu.VMEM((n_gx, MOST, width), BF16),
            pltpu.VMEM((n_gy, routes, 2 * share), BF16),
            pltpu.VMEM((n_gx, n_gy, MOST, 2 * share), BF16),
            pltpu.VMEM((n_gx, n_gy, MOST, 2 * share), BF16),
            pltpu.VMEM((n_gy, rows, hidden), BF16),
            pltpu.VMEM((n_gy, rows, hidden), BF16),
            pltpu.VMEM((n_gy, rows, hidden), BF16),
            pltpu.VMEM((n_gy, rows, hidden), F32),
            pltpu.VMEM((n_gy, rows, hidden), F32),
            dma,
            dma((n_gx,)), dma((n_gx,)), dma((n_gx,)), dma((n_gx,)),
            dma((n_gy,)), dma((n_gy,)),
            dma((n_gx,)), dma((n_gx,)),
            dma((n_gy,)), dma((n_gy,)), dma((n_gy,)), dma((n_gy,)),
        ],
        compiler_params=pltpu.CompilerParams(
            collective_id=0, has_side_effects=True, vmem_limit_bytes=67_043_328
        ),
        name="exchange",
    )(activations, out_grad, pre, ids, wt, down_weight[0])
    rows_act, rows_grad = rows_act.reshape(slots, width), rows_grad.reshape(slots, width)
    ha, gg, gu = (value.reshape(slots, hidden) for value in (ha, gg, gu))
    grad_gate = contract_rows(rows_act, gg)[None]
    grad_up = contract_rows(rows_act, gu)[None]
    grad_down = contract_rows(ha, rows_grad)[None]
    return (grad_gate, grad_up, grad_down)


def solution(mesh):
    placed = (
        P("gx", "gy"),
        P("gx", "gy"),
        P("gx", None, "gy"),
        P("gx", None, "gy"),
        P("gx", None),
        P("gx", None),
        P("gx", None, "gy"),
    )
    return jax.shard_map(
        on_device,
        mesh=mesh,
        in_specs=placed,
        out_specs=(P("gx", "gy", None), P("gx", "gy", None), P("gx", None, "gy")),
        check_vma=False,
    )
```

time: 146 us -> 86.2 us (0.59)
  the two profiles are of different devices: /device:TPU:6 before, /device:TPU:26 now
where the time goes in v1:
time: 86.2 us; the launch traced here: 86 us
  Pallas kernels  69.8 us (81%)
  matrix products  13.5 us (16%)
  other arithmetic  1.21 us (1%)
    pallas_call x1, Pallas kernels, on_device(): pl.pallas_call(functools.partial(exchange_kernel, n_gx, n_gy, top), out_s...  69.8 us
    dot_general x3, matrix products, contract_rows(): lax.dot_general(left, right, (((0,), (0,)), ((), ())), preferred_element_...  13.5 us

profile of v1, /device:TPU:26, one launch (start us, length us, event | category | flops | bytes accessed | tf_op | source)
XLA Modules:
  0.0 86.0 jit_solution(10046604437456307520)
XLA Ops:
  0.6 1.2 %maximum_bitcast_fusion = bf16[2,128,512]{2,0,1:T(2,128)(2,1)S(1)} fusion(bf16[128,2,256]{2,1,0:T(2,128)(2,1)} %param.10, bf16[128,2,256]{2,1,0:T(2,128)(2,1)} %param.9), kind=kLoop, calls=%fused_computation.6 | loop fusion | flops 524288 | bytes 524288 | tf_op jit(solution)/shard_map/transpose | solution.py:256
  1.8 0.7 copy.10
  2.6 69.8 %exchange.1 = (bf16[8,48,1792]{2,1,0:T(8,128)(2,1)}, bf16[8,48,1792]{2,1,0:T(8,128)(2,1)}, bf16[4,96,1024]{2,1,0:T(8,128)(2,1)}, bf16[4,96,1024]{2,1,0:T(8,128)(2,1)}, bf16[4,96,1024]{2,1,0:T(8,128)(2,1)}) custom-call(bf16[128,1792]{1,0:T(8,128)(2,1)} %act_ref.1, bf16[128,1792]{1,0:T(8,128)(2,1)} %grad_ref.1, bf16[256,512]{1,0:T(8,128)(2,1)} %bitcast.28, ...), custom_call_target="tpu_custom_call" | custom-call | tf_op jit(solution)/shard_map/exchange/pallas_call | solution.py:260
  72.4 0.0 copy-start.1
  72.4 0.0 copy-start.3
  72.4 5.6 %fusion = bf16[1,1792,1024]{2,1,0:T(8,128)(2,1)} fusion(bf16[384,1792]{1,0:T(8,128)(2,1)} %bitcast.32, bf16[384,1024]{1,0:T(8,128)(2,1)} %bitcast.36), kind=kOutput, calls=%fused_computation.3 | convolution fusion | flops 1411121152 | bytes 5832704 | tf_op jit(solution)/shard_map/dot_general | solution.py:17
  78.1 0.0 copy-done.1
  78.1 0.0 copy-done.3
  78.1 0.0 copy-start
  78.1 0.0 copy-start.2
  78.1 3.9 %fusion.1 = bf16[1,1792,1024]{2,1,0:T(8,128)(2,1)} fusion(bf16[384,1792]{1,0:T(8,128)(2,1)S(1)} %bitcast.33, bf16[384,1024]{1,0:T(8,128)(2,1)S(1)} %bitcast.35), kind=kOutput, calls=%fused_computation.4 | convolution fusion | flops 1411121152 | bytes 5832704 | tf_op jit(solution)/shard_map/dot_general | solution.py:17
  82.0 0.0 copy-done
  82.0 0.0 copy-done.2
  82.0 4.0 %fusion.2 = bf16[1,1024,1792]{2,1,0:T(8,128)(2,1)} fusion(bf16[384,1024]{1,0:T(8,128)(2,1)S(1)} %bitcast.34, bf16[384,1792]{1,0:T(8,128)(2,1)S(1)} %bitcast.31), kind=kOutput, calls=%fused_computation.5 | convolution fusion | flops 1411121152 | bytes 5832704 | tf_op jit(solution)/shard_map/dot_general | solution.py:17
Async XLA Ops:
  72.4 5.7 %copy-start.1 = (bf16[8,48,1792]{2,1,0:T(8,128)(2,1)S(1)}, bf16[8,48,1792]{2,1,0:T(8,128)(2,1)}, u32[]{:S(2)}) copy-start(bf16[8,48,1792]{2,1,0:T(8,128)(2,1)} %get-tuple-element.8) | copy-start | bytes 4128772
  72.4 5.7 %copy-start.3 = (bf16[4,96,1024]{2,1,0:T(8,128)(2,1)S(1)}, bf16[4,96,1024]{2,1,0:T(8,128)(2,1)}, u32[]{:S(2)}) copy-start(bf16[4,96,1024]{2,1,0:T(8,128)(2,1)} %get-tuple-element.10) | copy-start | bytes 2359300
  78.1 4.0 %copy-start = (bf16[8,48,1792]{2,1,0:T(8,128)(2,1)S(1)}, bf16[8,48,1792]{2,1,0:T(8,128)(2,1)}, u32[]{:S(2)}) copy-start(bf16[8,48,1792]{2,1,0:T(8,128)(2,1)} %get-tuple-element.12) | copy-start | bytes 4128772
  78.1 4.0 %copy-start.2 = (bf16[4,96,1024]{2,1,0:T(8,128)(2,1)S(1)}, bf16[4,96,1024]{2,1,0:T(8,128)(2,1)}, u32[]{:S(2)}) copy-start(bf16[4,96,1024]{2,1,0:T(8,128)(2,1)} %get-tuple-element.11) | copy-start | bytes 2359300

commit v2 on v1

--- a/solution.py
+++ b/solution.py
@@ -11,12 +11,6 @@
 F32 = jnp.float32
 BF16 = jnp.bfloat16
 MESH = pl.DeviceIdType.MESH
-
-
-def contract_rows(left, right):
-    return lax.dot_general(
-        left, right, (((0,), (0,)), ((), ())), preferred_element_type=jnp.float32
-    ).astype(jnp.bfloat16)
 
 
 def dot(left, right):
@@ -47,8 +41,6 @@
     part,
     part_in,
     hid,
-    fac_gate,
-    fac_up,
     down_sem,
     act_ss,
     act_rs,
@@ -84,6 +76,44 @@
             device_id={"gy": other}, device_id_type=MESH,
         )
 
+    def pass_on(src, buf, ss, rs, s, up, down):
+        if up:
+
+            @pl.when(my < n_gy - 1)
+            def _():
+                to_gy(src, buf.at[s], ss.at[s], rs.at[s], my + 1).start()
+
+        if down:
+
+            @pl.when(my > 0)
+            def _():
+                to_gy(src, buf.at[s], ss.at[n_gy + s], rs.at[s], my - 1).start()
+
+    def hop(buf, ss, rs, h):
+        below = jnp.maximum(my - h, 0)
+        above = jnp.minimum(my + h, n_gy - 1)
+
+        @pl.when(my >= h)
+        def _():
+            to_gy(buf.at[below], buf.at[below], ss.at[below], rs.at[below], my).wait_recv()
+            pass_on(buf.at[below], buf, ss, rs, below, True, False)
+
+        @pl.when(my + h < n_gy)
+        def _():
+            to_gy(buf.at[above], buf.at[above], ss.at[above], rs.at[above], my).wait_recv()
+            pass_on(buf.at[above], buf, ss, rs, above, False, True)
+
+    def drain(src, buf, ss, rs):
+        for s in range(n_gy):
+
+            @pl.when((my >= s) & (my < n_gy - 1))
+            def _():
+                to_gy(src, buf.at[s], ss.at[s], rs.at[s], my).wait_send()
+
+            @pl.when((my <= s) & (my > 0))
+            def _():
+                to_gy(src, buf.at[s], ss.at[n_gy + s], rs.at[s], my).wait_send()
+
     barrier = pltpu.get_barrier_semaphore()
     for d in range(1, n_gx):
         pl.semaphore_signal(
@@ -97,9 +127,7 @@
     down_copy.start()
     pl.semaphore_wait(barrier, n_gx - 1 + n_gy - 1)
 
-    for d in range(1, n_gy):
-        other = lax.rem(my + d, n_gy)
-        to_gy(pre_ref, pre_all.at[my], all_ss.at[d], all_rs.at[my], other).start()
+    pass_on(pre_ref, pre_all, all_ss, all_rs, my, True, True)
     pre_all[my] = pre_ref[...]
 
     ids = ids_ref[...]
@@ -178,9 +206,11 @@
         def _():
             part_in[my] = part[q]
 
-    for d in range(1, n_gy):
-        other = lax.rem(my + d, n_gy)
-        to_gy(pre_ref, pre_all.at[other], all_ss.at[0], all_rs.at[other], my).wait_recv()
+        if i + 1 < n_gy - 1:
+            hop(pre_all, all_ss, all_rs, i + 1)
+
+    if n_gy > 1:
+        hop(pre_all, all_ss, all_rs, n_gy - 1)
     for y in range(n_gy):
         pre_send[:, y] = (
             dot(pick, pre_all[y]).astype(BF16).reshape(n_gx, MOST, 2 * share)
@@ -199,31 +229,26 @@
     for y in range(1, n_gy):
         total = total + part_in[y].astype(F32)
     hid[my] = total.astype(BF16)
-    for d in range(1, n_gy):
-        other = lax.rem(my + d, n_gy)
-        to_gy(hid.at[my], hid.at[my], hid_ss.at[d], hid_rs.at[my], other).start()
+    pass_on(hid.at[my], hid, hid_ss, hid_rs, my, True, True)
+    for h in range(1, n_gy):
+        hop(hid, hid_ss, hid_rs, h)
 
     for d in range(1, n_gx):
         other = lax.rem(me + d, n_gx)
         to_gx(pre_send.at[0], pre_rows.at[other], pre_ss.at[0], pre_rs.at[other], me).wait_recv()
-    for q in range(n_gy):
+
+    @pl.loop(0, n_gy)
+    def _(q):
         for y in range(n_gy):
-            both = pre_rows[q * per : (q + 1) * per, y].reshape(block, 2 * share).astype(F32)
+            both = pre_rows[pl.ds(q * per, per), y].reshape(block, 2 * share).astype(F32)
             gate, up = both[:, :share], both[:, share:]
             sig = jax.nn.sigmoid(gate)
             silu = gate * sig
             cols = slice(y * share, (y + 1) * share)
+            value = hid[q, :, cols].astype(F32)
             ha_ref[q, :, cols] = (silu * up).astype(BF16)
-            fac_up[q, :, cols] = silu
-            fac_gate[q, :, cols] = up * sig * (1.0 + gate * (1.0 - sig))
-
-    for d in range(1, n_gy):
-        other = lax.rem(my + d, n_gy)
-        to_gy(hid.at[0], hid.at[other], hid_ss.at[0], hid_rs.at[other], my).wait_recv()
-    for q in range(n_gy):
-        value = hid[q].astype(F32)
-        gg_ref[q] = (value * fac_gate[q]).astype(BF16)
-        gu_ref[q] = (value * fac_up[q]).astype(BF16)
+            gg_ref[q, :, cols] = (value * up * sig * (1.0 + gate * (1.0 - sig))).astype(BF16)
+            gu_ref[q, :, cols] = (value * silu).astype(BF16)
 
     for d in range(1, n_gx):
         other = lax.rem(me + d, n_gx)
@@ -238,9 +263,46 @@
             to_gx(src.at[other], dst.at[me], ss.at[d], rs.at[me], other).wait_send()
     for d in range(1, n_gy):
         other = lax.rem(my + d, n_gy)
-        to_gy(pre_ref, pre_all.at[my], all_ss.at[d], all_rs.at[my], other).wait_send()
         to_gy(part.at[other], part_in.at[my], part_ss.at[other], part_rs.at[my], other).wait_send()
-        to_gy(hid.at[my], hid.at[my], hid_ss.at[d], hid_rs.at[my], other).wait_send()
+    drain(pre_ref, pre_all, all_ss, all_rs)
+    drain(hid.at[0], hid, hid_ss, hid_rs)
+
+
+def product_kernel(act_ref, grad_ref, ha_ref, gg_ref, gu_ref, gate_ref, up_ref, down_ref, turned):
+    @pl.when(pl.program_id(0) == 0)
+    def _():
+        turned[...] = ha_ref[...].T
+
+    act = act_ref[...].T
+    gate_ref[...] = dot(act, gg_ref[...]).astype(BF16)
+    up_ref[...] = dot(act, gu_ref[...]).astype(BF16)
+    down_ref[...] = dot(turned[...], grad_ref[...]).astype(BF16)
+
+
+def products(rows_act, rows_grad, ha, gg, gu):
+    slots, width = rows_act.shape
+    hidden = ha.shape[1]
+    tile = 256 if width % 256 == 0 else width
+    wide = pl.BlockSpec((slots, tile), lambda i: (0, i))
+    whole = pl.BlockSpec((slots, hidden), lambda i: (0, 0), pipeline_mode=pl.Buffered(1))
+    tall = pl.BlockSpec((None, tile, hidden), lambda i: (0, i, 0))
+    flat = pl.BlockSpec((None, hidden, tile), lambda i: (0, 0, i))
+    return pl.pallas_call(
+        product_kernel,
+        grid=(width // tile,),
+        out_shape=(
+            jax.ShapeDtypeStruct((1, width, hidden), BF16),
+            jax.ShapeDtypeStruct((1, width, hidden), BF16),
+            jax.ShapeDtypeStruct((1, hidden, width), BF16),
+        ),
+        in_specs=[wide, wide, whole, whole, whole],
+        out_specs=(tall, tall, flat),
+        scratch_shapes=[pltpu.VMEM((hidden, slots), BF16)],
+        compiler_params=pltpu.CompilerParams(
+            dimension_semantics=("arbitrary",), vmem_limit_bytes=40 * 1024 * 1024
+        ),
+        name="products",
+    )(rows_act, rows_grad, ha, gg, gu)
 
 
 def on_device(activations, out_grad, saved_gate, saved_up, route_ids, route_weight, down_weight):
@@ -278,13 +340,11 @@
             pltpu.VMEM((n_gy, rows, hidden), BF16),
             pltpu.VMEM((n_gy, rows, hidden), BF16),
             pltpu.VMEM((n_gy, rows, hidden), BF16),
-            pltpu.VMEM((n_gy, rows, hidden), F32),
-            pltpu.VMEM((n_gy, rows, hidden), F32),
             dma,
             dma((n_gx,)), dma((n_gx,)), dma((n_gx,)), dma((n_gx,)),
-            dma((n_gy,)), dma((n_gy,)),
+            dma((2 * n_gy,)), dma((n_gy,)),
             dma((n_gx,)), dma((n_gx,)),
-            dma((n_gy,)), dma((n_gy,)), dma((n_gy,)), dma((n_gy,)),
+            dma((n_gy,)), dma((n_gy,)), dma((2 * n_gy,)), dma((n_gy,)),
         ],
         compiler_params=pltpu.CompilerParams(
             collective_id=0, has_side_effects=True, vmem_limit_bytes=67_043_328
@@ -293,10 +353,7 @@
     )(activations, out_grad, pre, ids, wt, down_weight[0])
     rows_act, rows_grad = rows_act.reshape(slots, width), rows_grad.reshape(slots, width)
     ha, gg, gu = (value.reshape(slots, hidden) for value in (ha, gg, gu))
-    grad_gate = contract_rows(rows_act, gg)[None]
-    grad_up = contract_rows(rows_act, gu)[None]
-    grad_down = contract_rows(ha, rows_grad)[None]
-    return (grad_gate, grad_up, grad_down)
+    return tuple(products(rows_act, rows_grad, ha, gg, gu))
 
 
 def solution(mesh):

time: 86.2 us -> 86.5 us (level)
  the two profiles are of different devices: /device:TPU:26 before, /device:TPU:6 now
where the time goes in v2:
time: 86.5 us; the launch traced here: 86.1 us
  Pallas kernels  77.4 us (89%)
  local copies, waits for them, and re-layouts  6.8 us (8%)
  other arithmetic  1.21 us (1%)
    pallas_call x1, Pallas kernels, on_device(): pl.pallas_call(functools.partial(exchange_kernel, n_gx, n_gy, top), out_s...  68.9 us
    pallas_call x1, Pallas kernels, products(): pl.pallas_call(product_kernel, grid=(width // tile,), out_shape=(jax.Shap...  8.52 us
    unnamed x10, local copies, waits for them, and re-layouts  6.07 us

profile of v2, /device:TPU:6, one launch (start us, length us, event | category | flops | bytes accessed | tf_op | source)
XLA Modules:
  0.0 86.1 jit_solution(10256439917376470945)
XLA Ops:
  0.6 1.2 %maximum_bitcast_fusion = bf16[2,128,512]{2,0,1:T(2,128)(2,1)S(1)} fusion(bf16[128,2,256]{2,1,0:T(2,128)(2,1)} %param.10, bf16[128,2,256]{2,1,0:T(2,128)(2,1)} %param.9), kind=kLoop, calls=%fused_computation | loop fusion | flops 524288 | bytes 524288 | tf_op jit(solution)/shard_map/transpose | solution.py:318
  1.8 0.7 copy.10
  2.6 68.9 %exchange.1 = (bf16[8,48,1792]{2,1,0:T(8,128)(2,1)}, bf16[8,48,1792]{2,1,0:T(8,128)(2,1)}, bf16[4,96,1024]{2,1,0:T(8,128)(2,1)}, bf16[4,96,1024]{2,1,0:T(8,128)(2,1)}, bf16[4,96,1024]{2,1,0:T(8,128)(2,1)}) custom-call(bf16[128,1792]{1,0:T(8,128)(2,1)} %act_ref.1, bf16[128,1792]{1,0:T(8,128)(2,1)} %grad_ref.1, bf16[256,512]{1,0:T(8,128)(2,1)} %bitcast.21, ...), custom_call_target="tpu_custom_call" | custom-call | tf_op jit(solution)/shard_map/exchange/pallas_call | solution.py:322
  71.5 0.0 copy-start
  71.5 1.3 %copy-done = bf16[8,48,1792]{2,1,0:T(8,128)(2,1)S(1)} copy-done((bf16[8,48,1792]{2,1,0:T(8,128)(2,1)S(1)}, bf16[8,48,1792]{2,1,0:T(8,128)(2,1)}, u32[]{:S(2)}) %copy-start) | copy-done | bytes 1376280
  72.8 0.0 copy-start.1
  72.9 1.3 %copy-done.1 = bf16[8,48,1792]{2,1,0:T(8,128)(2,1)S(1)} copy-done((bf16[8,48,1792]{2,1,0:T(8,128)(2,1)S(1)}, bf16[8,48,1792]{2,1,0:T(8,128)(2,1)}, u32[]{:S(2)}) %copy-start.1) | copy-done | bytes 1376280
  74.2 0.0 copy-start.2
  74.2 1.1 %copy-done.2 = bf16[4,96,1024]{2,1,0:T(8,128)(2,1)S(1)} copy-done((bf16[4,96,1024]{2,1,0:T(8,128)(2,1)S(1)}, bf16[4,96,1024]{2,1,0:T(8,128)(2,1)}, u32[]{:S(2)}) %copy-start.2) | copy-done | bytes 786456
  75.3 0.0 copy-start.3
  75.3 1.1 %copy-done.3 = bf16[4,96,1024]{2,1,0:T(8,128)(2,1)S(1)} copy-done((bf16[4,96,1024]{2,1,0:T(8,128)(2,1)S(1)}, bf16[4,96,1024]{2,1,0:T(8,128)(2,1)}, u32[]{:S(2)}) %copy-start.3) | copy-done | bytes 786456
  76.5 0.0 copy-start.4
  76.5 1.1 %copy-done.4 = bf16[4,96,1024]{2,1,0:T(8,128)(2,1)S(1)} copy-done((bf16[4,96,1024]{2,1,0:T(8,128)(2,1)S(1)}, bf16[4,96,1024]{2,1,0:T(8,128)(2,1)}, u32[]{:S(2)}) %copy-start.4) | copy-done | bytes 786456
  77.6 8.5 %products.1 = (bf16[1,1792,1024]{2,1,0:T(8,128)(2,1)}, bf16[1,1792,1024]{2,1,0:T(8,128)(2,1)}, bf16[1,1024,1792]{2,1,0:T(8,128)(2,1)}) custom-call(bf16[384,1792]{1,0:T(8,128)(2,1)S(1)} %bitcast.15, bf16[384,1792]{1,0:T(8,128)(2,1)S(1)} %bitcast.16, bf16[384,1024]{1,0:T(8,128)(2,1)S(1)} %bitcast.17, bf16[384,1024]{1,0:T(8,128)(2,1)S(1)} %bitcast.18, ...), custom_call_target="tpu_custom_call" | custom-call | tf_op jit(solution)/shard_map/products/pallas_call | solution.py:290
Async XLA Ops:
  71.5 1.3 %copy-start = (bf16[8,48,1792]{2,1,0:T(8,128)(2,1)S(1)}, bf16[8,48,1792]{2,1,0:T(8,128)(2,1)}, u32[]{:S(2)}) copy-start(bf16[8,48,1792]{2,1,0:T(8,128)(2,1)} %get-tuple-element.8) | copy-start | bytes 4128772
  72.8 1.3 %copy-start.1 = (bf16[8,48,1792]{2,1,0:T(8,128)(2,1)S(1)}, bf16[8,48,1792]{2,1,0:T(8,128)(2,1)}, u32[]{:S(2)}) copy-start(bf16[8,48,1792]{2,1,0:T(8,128)(2,1)} %get-tuple-element.9) | copy-start | bytes 4128772
  74.2 1.1 %copy-start.2 = (bf16[4,96,1024]{2,1,0:T(8,128)(2,1)S(1)}, bf16[4,96,1024]{2,1,0:T(8,128)(2,1)}, u32[]{:S(2)}) copy-start(bf16[4,96,1024]{2,1,0:T(8,128)(2,1)} %get-tuple-element.10) | copy-start | bytes 2359300
  75.3 1.1 %copy-start.3 = (bf16[4,96,1024]{2,1,0:T(8,128)(2,1)S(1)}, bf16[4,96,1024]{2,1,0:T(8,128)(2,1)}, u32[]{:S(2)}) copy-start(bf16[4,96,1024]{2,1,0:T(8,128)(2,1)} %get-tuple-element.11) | copy-start | bytes 2359300
  76.5 1.1 %copy-start.4 = (bf16[4,96,1024]{2,1,0:T(8,128)(2,1)S(1)}, bf16[4,96,1024]{2,1,0:T(8,128)(2,1)}, u32[]{:S(2)}) copy-start(bf16[4,96,1024]{2,1,0:T(8,128)(2,1)} %get-tuple-element.12) | copy-start | bytes 2359300

commit v3 on v2

--- a/solution.py
+++ b/solution.py
@@ -299,7 +299,7 @@
         out_specs=(tall, tall, flat),
         scratch_shapes=[pltpu.VMEM((hidden, slots), BF16)],
         compiler_params=pltpu.CompilerParams(
-            dimension_semantics=("arbitrary",), vmem_limit_bytes=40 * 1024 * 1024
+            dimension_semantics=("arbitrary",), vmem_limit_bytes=67_043_328
         ),
         name="products",
     )(rows_act, rows_grad, ha, gg, gu)

time: 86.5 us -> 82.4 us (0.953)
  local copies, waits for them, and re-layouts: 6.8 us -> 0.73 us
  Pallas kernels: 77.4 us -> 79.5 us
    unnamed x10 -> x0, local copies, waits for them, and re-layouts: 6.07 us -> none
    pallas_call x1, Pallas kernels: 8.52 us -> 10.6 us  [products(): pl.pallas_call(product_kernel, grid=(width // tile,), out_shape=(jax.Shap...]
where the time goes in v3:
time: 82.4 us; the launch traced here: 82.1 us
  Pallas kernels  79.5 us (96%)
  other arithmetic  1.21 us (1%)
    pallas_call x1, Pallas kernels, on_device(): pl.pallas_call(functools.partial(exchange_kernel, n_gx, n_gy, top), out_s...  68.9 us
    pallas_call x1, Pallas kernels, products(): pl.pallas_call(product_kernel, grid=(width // tile,), out_shape=(jax.Shap...  10.6 us

profile of v3, /device:TPU:6, one launch (start us, length us, event | category | flops | bytes accessed | tf_op | source)
XLA Modules:
  0.0 82.1 jit_solution(10568161005689138555)
XLA Ops:
  0.6 1.2 %maximum_bitcast_fusion = bf16[2,128,512]{2,0,1:T(2,128)(2,1)S(1)} fusion(bf16[128,2,256]{2,1,0:T(2,128)(2,1)} %param.10, bf16[128,2,256]{2,1,0:T(2,128)(2,1)} %param.9), kind=kLoop, calls=%fused_computation | loop fusion | flops 524288 | bytes 524288 | tf_op jit(solution)/shard_map/transpose | solution.py:318
  1.8 0.7 copy.10
  2.6 68.9 %exchange.1 = (bf16[8,48,1792]{2,1,0:T(8,128)(2,1)}, bf16[8,48,1792]{2,1,0:T(8,128)(2,1)}, bf16[4,96,1024]{2,1,0:T(8,128)(2,1)}, bf16[4,96,1024]{2,1,0:T(8,128)(2,1)}, bf16[4,96,1024]{2,1,0:T(8,128)(2,1)}) custom-call(bf16[128,1792]{1,0:T(8,128)(2,1)} %act_ref.1, bf16[128,1792]{1,0:T(8,128)(2,1)} %grad_ref.1, bf16[256,512]{1,0:T(8,128)(2,1)} %bitcast.18, ...), custom_call_target="tpu_custom_call" | custom-call | tf_op jit(solution)/shard_map/exchange/pallas_call | solution.py:322
  71.5 10.6 %products.1 = (bf16[1,1792,1024]{2,1,0:T(8,128)(2,1)}, bf16[1,1792,1024]{2,1,0:T(8,128)(2,1)}, bf16[1,1024,1792]{2,1,0:T(8,128)(2,1)}) custom-call(bf16[384,1792]{1,0:T(8,128)(2,1)} %bitcast.16, bf16[384,1792]{1,0:T(8,128)(2,1)} %bitcast.17, bf16[384,1024]{1,0:T(8,128)(2,1)} %bitcast.19, bf16[384,1024]{1,0:T(8,128)(2,1)} %bitcast.20, bf16[384,1024]{1,0:T(8,128)(2,1)} %bitcast.21), custom_call_target="tpu_custom_call" | custom-call | tf_op jit(solution)/shard_map/products/pallas_call | solution.py:290
